TPU v7x, 32 devices: a whole 2x2x4 slice. The times are simulated.
32 devices in a mesh: batch: 8 (over z, x), seq: 4 (over y, core).
Axes of the slice: x: 2, y: 2, z: 4, core: 2. Of those that a mesh axis runs over, the one named last changes fastest.
Arguments:
- tokens: bfloat16 [8, 1024, 1024], P('batch', 'seq'), may hold values from -6 to 6
- cotangent: bfloat16 [8, 1024, 1024], P('batch', 'seq'), may hold values from -6 to 6
- image_tokens: bfloat16 [8, 1025, 768], P('batch'), may hold values from -6 to 6
- image_lengths: int32 [8], P('batch'), may hold values from 512 to 1025, as said below
- key_mask: int32 [8, 1025], P('batch'), may hold values 0 or 1
- camera: bfloat16 [8, 1024], P(None, 'batch'), may hold values from -6 to 6
- modulation: bfloat16 [1024, 6144], P('batch'), may hold values from -0.1875 to 0.1875
- q_cross: bfloat16 [1024, 1024], P('batch'), may hold values from -0.1875 to 0.1875
- kv_image: bfloat16 [768, 2048], P('batch'), may hold values from -0.21875 to 0.21875
- out_cross: bfloat16 [1024, 1024], P('batch'), may hold values from -3.5 to 3.5
- qkv_self: bfloat16 [1024, 3072], P('batch'), may hold values from -0.1875 to 0.1875
- out_self: bfloat16 [1024, 1024], P('batch'), may hold values from -6 to 6
- mlp_in: bfloat16 [1024, 4096], P('batch'), may hold values from -0.1875 to 0.1875
- mlp_out: bfloat16 [4096, 1024], P('batch'), may hold values from -0.09375 to 0.09375
Outputs:
- output: bfloat16 [8, 1024, 1024], P('batch', 'seq')
- grad_tokens: float32 [8, 1024, 1024], P('batch', 'seq')
- grad_modulation: float32 [1024, 6144], P('batch')
- grad_q_cross: float32 [1024, 1024], P('batch')
- grad_kv_image: float32 [768, 2048], P('batch')
- grad_out_cross: float32 [1024, 1024], P('batch')
- grad_qkv_self: float32 [1024, 3072], P('batch')
- grad_out_self: float32 [1024, 1024], P('batch')
- grad_mlp_in: float32 [1024, 4096], P('batch')
- grad_mlp_out: float32 [4096, 1024], P('batch')
Inputs may be any that keep to these rules, and one draw needn't show every extreme that they name: `image_lengths`: some object has 1025 valid image tokens and some has 512.
All inputs are finite; a program needn't handle non-finite values. No bound on the sum of `key_mask` on one device may be relied on, other than what follows from the above.
Results may differ from a plain program's by a relative error of at most 0.025.
The roundings to bfloat16 on the way count: a program that leaves them out, or rounds other values in their place, can miss the bound.
Values may be sent and summed in bfloat16 or wider, within the bound.
A program may use at most 256 MiB of HBM per device.

v0:
```python
import jax
import jax.numpy as jnp
from jax import lax
from jax.sharding import PartitionSpec as P

HEADS = 16
HEAD_DIM = 64


epsilon = 1e-06
group_heads = 4
highest = lax.Precision.HIGHEST


def modulated_norm(values, shift, scale):
    center = values - jnp.mean(values, axis=-1, keepdims=True)
    normed = center * lax.rsqrt(jnp.mean(center * center, axis=-1, keepdims=True) + epsilon)
    return normed * (1.0 + scale) + shift


def product(left, right):
    return jnp.dot(left, right, preferred_element_type=jnp.float32)


def contract_rows(left, right):
    return lax.dot_general(
        left, right, (((0,), (0,)), ((), ())), preferred_element_type=jnp.float32
    )


def times_transposed(left, right):
    return lax.dot_general(
        left, right, (((1,), (1,)), ((), ())), preferred_element_type=jnp.float32
    )


def split_heads(values):
    rows = values.shape[0]
    grouped = values.reshape(rows, HEADS // group_heads, group_heads, HEAD_DIM)
    return grouped.transpose(1, 2, 0, 3)


def join_heads(values):
    groups, inner, rows, depth = values.shape
    return values.transpose(2, 0, 1, 3).reshape(rows, groups * inner * depth)


def scores_of(query_group, key_group, valid):
    scores = jnp.einsum(
        "hqd,hkd->hqk", query_group, key_group, preferred_element_type=jnp.float32
    ) * HEAD_DIM ** (-0.5)
    return jnp.where(valid[None, None, :], scores, -1000000000.0)


def attend_forward(query, key_rows, value_rows, valid):

    def one_group(pieces):
        query_group, key_group, value_group = pieces
        scores = scores_of(query_group, key_group, valid)
        top = jnp.max(scores, axis=-1, keepdims=True)
        expo = jnp.exp(scores - top)
        total = jnp.sum(expo, axis=-1, keepdims=True)
        probs = (expo / total).astype(jnp.bfloat16)
        result = jnp.einsum("hqk,hkd->hqd", probs, value_group, preferred_element_type=jnp.float32)
        return (result, top, total)

    results, tops, totals = lax.map(
        one_group, (split_heads(query), split_heads(key_rows), split_heads(value_rows))
    )
    return (join_heads(results), (tops, totals))


def attend_backward(query, key_rows, value_rows, valid, stats, grad_output):
    tops, totals = stats

    def one_group(pieces):
        query_group, key_group, value_group, top, total, grad_group = pieces
        scores = scores_of(query_group, key_group, valid)
        probs = jnp.exp(scores - top) / total
        grad_probs = jnp.einsum(
            "hqd,hkd->hqk", grad_group, value_group, preferred_element_type=jnp.float32
        )
        inner = jnp.sum(probs * grad_probs, axis=-1, keepdims=True)
        grad_scores = (probs * (grad_probs - inner)).astype(jnp.bfloat16)
        factor = HEAD_DIM ** (-0.5)
        grad_query = (
            jnp.einsum("hqk,hkd->hqd", grad_scores, key_group, preferred_element_type=jnp.float32)
            * factor
        )
        grad_keys = (
            jnp.einsum("hqk,hqd->hkd", grad_scores, query_group, preferred_element_type=jnp.float32)
            * factor
        )
        grad_values = jnp.einsum(
            "hqk,hqd->hkd",
            probs.astype(jnp.bfloat16),
            grad_group,
            preferred_element_type=jnp.float32,
        )
        return (grad_query, inner, grad_keys, grad_values)

    results = lax.map(
        one_group,
        (
            split_heads(query),
            split_heads(key_rows),
            split_heads(value_rows),
            tops,
            totals,
            split_heads(grad_output),
        ),
    )
    return (join_heads(results[0]), results[1], join_heads(results[2]), join_heads(results[3]))


def local(
    tokens,
    cotangent,
    image_tokens,
    image_lengths,
    key_mask,
    camera,
    modulation,
    q_cross,
    kv_image,
    out_cross,
    qkv_self,
    out_self,
    mlp_in,
    mlp_out,
):
    q_full, kv_full, out_cross_full, qkv_full, out_self_full, mlp_in_full, mlp_out_full = (
        lax.all_gather(q_cross, "batch", axis=0, tiled=True),
        lax.all_gather(kv_image, "batch", axis=0, tiled=True),
        lax.all_gather(out_cross, "batch", axis=0, tiled=True),
        lax.all_gather(qkv_self, "batch", axis=0, tiled=True),
        lax.all_gather(out_self, "batch", axis=0, tiled=True),
        lax.all_gather(mlp_in, "batch", axis=0, tiled=True),
        lax.all_gather(mlp_out, "batch", axis=0, tiled=True),
    )
    camera_gate = jax.nn.silu(camera.astype(jnp.float32)).astype(jnp.bfloat16)
    modulation_all = lax.psum(product(camera_gate, modulation), "batch")
    object_index = lax.axis_index("batch")
    width = tokens.shape[2]
    shifts = lax.dynamic_index_in_dim(modulation_all, object_index, 0, keepdims=False).reshape(
        6, width
    )
    stream = tokens[0].astype(jnp.float32)
    image_rows = image_tokens[0]
    positions = jnp.arange(image_rows.shape[0], dtype=jnp.int32)
    valid = (positions < image_lengths[0]) & ((key_mask[0] == 1) | (positions == 0))
    everywhere = jnp.ones((lax.axis_size("seq") * stream.shape[0],), dtype=jnp.bool_)
    normed_cross, cross_pullback = jax.vjp(modulated_norm, stream, shifts[0], shifts[1])
    normed_cross = normed_cross.astype(jnp.bfloat16)
    query_cross = product(normed_cross, q_full).astype(jnp.bfloat16)
    image_kv = product(image_rows, kv_full)
    image_keys = image_kv[:, :width].astype(jnp.bfloat16)
    image_values = image_kv[:, width:].astype(jnp.bfloat16)
    attended_cross, cross_stats = attend_forward(query_cross, image_keys, image_values, valid)
    attended_cross = attended_cross.astype(jnp.bfloat16)
    after_cross = stream + product(attended_cross, out_cross_full)
    normed_self, self_pullback = jax.vjp(modulated_norm, after_cross, shifts[2], shifts[3])
    normed_self = normed_self.astype(jnp.bfloat16)
    packed = product(normed_self, qkv_full).astype(jnp.bfloat16)
    query_self = packed[:, :width]
    key_local = packed[:, width : 2 * width]
    value_local = packed[:, 2 * width :]
    key_whole, value_whole = (
        lax.all_gather(key_local, "seq", axis=0, tiled=True),
        lax.all_gather(value_local, "seq", axis=0, tiled=True),
    )
    attended_self, self_stats = attend_forward(query_self, key_whole, value_whole, everywhere)
    attended_self = attended_self.astype(jnp.bfloat16)
    after_self = after_cross + product(attended_self, out_self_full)
    normed_mlp, mlp_pullback = jax.vjp(modulated_norm, after_self, shifts[4], shifts[5])
    normed_mlp = normed_mlp.astype(jnp.bfloat16)
    up_rows = product(normed_mlp, mlp_in_full)
    hidden, gelu_pullback = jax.vjp(jax.nn.gelu, up_rows)
    hidden = hidden.astype(jnp.bfloat16)
    output = after_self + product(hidden, mlp_out_full)
    grad_stream = cotangent[0].astype(jnp.float32)
    grad_branch = grad_stream.astype(jnp.bfloat16)
    grad_mlp_out = contract_rows(hidden, grad_branch)
    (grad_up,) = gelu_pullback(times_transposed(grad_branch, mlp_out_full))
    grad_up = grad_up.astype(jnp.bfloat16)
    grad_mlp_in = contract_rows(normed_mlp, grad_up)
    grad_from, shift_mlp, scale_mlp = mlp_pullback(times_transposed(grad_up, mlp_in_full))
    grad_stream = grad_stream + grad_from
    grad_branch = grad_stream.astype(jnp.bfloat16)
    grad_out_self = contract_rows(attended_self, grad_branch)
    grad_attended = times_transposed(grad_branch, out_self_full).astype(jnp.bfloat16)
    grad_query, inner_local, key_terms, value_terms = attend_backward(
        query_self, key_whole, value_whole, everywhere, self_stats, grad_attended
    )
    grad_key, grad_value = (
        lax.psum_scatter(key_terms, "seq", scatter_dimension=0, tiled=True),
        lax.psum_scatter(value_terms, "seq", scatter_dimension=0, tiled=True),
    )
    grad_packed = jnp.concatenate([grad_query, grad_key, grad_value], axis=1).astype(jnp.bfloat16)
    grad_qkv_self = contract_rows(normed_self, grad_packed)
    grad_from, shift_self, scale_self = self_pullback(times_transposed(grad_packed, qkv_full))
    grad_stream = grad_stream + grad_from
    grad_branch = grad_stream.astype(jnp.bfloat16)
    grad_out_cross = contract_rows(attended_cross, grad_branch)
    grad_attended = times_transposed(grad_branch, out_cross_full).astype(jnp.bfloat16)
    grad_query, inner_cross, key_terms, value_terms = attend_backward(
        query_cross, image_keys, image_values, valid, cross_stats, grad_attended
    )
    image_float = image_rows.astype(jnp.float32)
    image_key_grad, image_value_grad = (
        lax.psum_scatter(
            key_terms.astype(jnp.bfloat16), "seq", scatter_dimension=1, tiled=True
        ).astype(jnp.float32),
        lax.psum_scatter(
            value_terms.astype(jnp.bfloat16), "seq", scatter_dimension=1, tiled=True
        ).astype(jnp.float32),
    )
    block_width = image_key_grad.shape[1]
    column_start = lax.axis_index("seq") * block_width
    image_grads = jnp.concatenate([image_key_grad, image_value_grad], axis=1)
    kv_block = lax.dot_general(
        image_float,
        image_grads,
        (((0,), (0,)), ((), ())),
        precision=highest,
        preferred_element_type=jnp.float32,
    )
    grad_kv_image = jnp.zeros((image_rows.shape[1], 2 * width), jnp.float32)
    grad_kv_image = lax.dynamic_update_slice(
        grad_kv_image, kv_block[:, :block_width], (jnp.int32(0), column_start)
    )
    grad_kv_image = lax.dynamic_update_slice(
        grad_kv_image, kv_block[:, block_width:], (jnp.int32(0), column_start + width)
    )
    grad_query = grad_query.astype(jnp.bfloat16)
    grad_q_cross = contract_rows(normed_cross, grad_query)
    grad_from, shift_cross, scale_cross = cross_pullback(times_transposed(grad_query, q_full))
    grad_input = grad_stream + grad_from
    grad_row = jnp.concatenate(
        [shift_cross, scale_cross, shift_self, scale_self, shift_mlp, scale_mlp]
    )
    grad_table = lax.dynamic_update_slice(
        jnp.zeros(modulation_all.shape, jnp.float32),
        grad_row[None, :],
        (object_index, jnp.int32(0)),
    )
    grad_table = lax.psum(grad_table, ("batch", "seq"))
    grad_modulation = lax.dot_general(
        camera_gate.astype(jnp.float32),
        grad_table,
        (((0,), (0,)), ((), ())),
        precision=highest,
        preferred_element_type=jnp.float32,
    )
    terms = (
        grad_q_cross,
        grad_kv_image,
        grad_out_cross,
        grad_qkv_self,
        grad_out_self,
        grad_mlp_in,
        grad_mlp_out,
    )
    shares = (
        lax.psum_scatter(
            terms[0].astype(jnp.bfloat16), "batch", scatter_dimension=0, tiled=True
        ).astype(jnp.float32),
        lax.psum_scatter(
            terms[1].astype(jnp.bfloat16), "batch", scatter_dimension=0, tiled=True
        ).astype(jnp.float32),
        lax.psum_scatter(
            terms[2].astype(jnp.bfloat16), "batch", scatter_dimension=0, tiled=True
        ).astype(jnp.float32),
        lax.psum_scatter(
            terms[3].astype(jnp.bfloat16), "batch", scatter_dimension=0, tiled=True
        ).astype(jnp.float32),
        lax.psum_scatter(
            terms[4].astype(jnp.bfloat16), "batch", scatter_dimension=0, tiled=True
        ).astype(jnp.float32),
        lax.psum_scatter(
            terms[5].astype(jnp.bfloat16), "batch", scatter_dimension=0, tiled=True
        ).astype(jnp.float32),
        lax.psum_scatter(
            terms[6].astype(jnp.bfloat16), "batch", scatter_dimension=0, tiled=True
        ).astype(jnp.float32),
    )
    totals = (
        lax.psum(shares[0].astype(jnp.bfloat16), "seq").astype(jnp.float32),
        lax.psum(shares[1].astype(jnp.bfloat16), "seq").astype(jnp.float32),
        lax.psum(shares[2].astype(jnp.bfloat16), "seq").astype(jnp.float32),
        lax.psum(shares[3].astype(jnp.bfloat16), "seq").astype(jnp.float32),
        lax.psum(shares[4].astype(jnp.bfloat16), "seq").astype(jnp.float32),
        lax.psum(shares[5].astype(jnp.bfloat16), "seq").astype(jnp.float32),
        lax.psum(shares[6].astype(jnp.bfloat16), "seq").astype(jnp.float32),
    )
    return (
        output.astype(jnp.bfloat16)[None],
        grad_input[None],
        grad_modulation,
        totals[0],
        totals[1],
        totals[2],
        totals[3],
        totals[4],
        totals[5],
        totals[6],
    )


def solution(mesh):
    return jax.shard_map(
        local,
        mesh=mesh,
        in_specs=(
            P("batch", "seq", None),
            P("batch", "seq", None),
            P("batch", None, None),
            P("batch"),
            P("batch", None),
            P(None, "batch"),
            P("batch", None),
            P("batch", None),
            P("batch", None),
            P("batch", None),
            P("batch", None),
            P("batch", None),
            P("batch", None),
            P("batch", None),
        ),
        out_specs=(
            P("batch", "seq", None),
            P("batch", "seq", None),
            P("batch", None),
            P("batch", None),
            P("batch", None),
            P("batch", None),
            P("batch", None),
            P("batch", None),
            P("batch", None),
            P("batch", None),
        ),
        check_vma=False,
    )
```

profile of v0, /device:TPU:17, one launch (start us, length us, event | category | flops | bytes accessed | tf_op | source)
XLA Modules:
  0.0 1924.3 jit_solution(18248695921334428257)
XLA Ops:
  15.5 64.7 %all-reduce.5.cloned.1.call-done = f32[8,6144]{1,0:T(8,128)} async-done(((f32[8,6144]{1,0:T(8,128)}), f32[8,6144]{1,0:T(8,128)}) %all-reduce.5.cloned.1.call-update) | async-done | bytes 196624 | tf_op jit(solution)/shard_map/psum | solution.py:142
  81.1 51.6 %all-gather.10.cloned.1.call-done = bf16[1024,1024]{1,0:T(8,128)(2,1)} async-done(((bf16[128,1024]{1,0:T(8,128)(2,1)}), bf16[1024,1024]{1,0:T(8,128)(2,1)}) %all-gather.10.cloned.1.call-update) | async-done | bytes 2097168 | tf_op jit(solution)/shard_map/all_gather | solution.py:133
  135.3 58.7 %all-gather.12.cloned.1.call-done = bf16[768,2048]{1,0:T(8,128)(2,1)} async-done(((bf16[96,2048]{1,0:T(8,128)(2,1)}), bf16[768,2048]{1,0:T(8,128)(2,1)}) %all-gather.12.cloned.1.call-update) | async-done | bytes 3145744 | tf_op jit(solution)/shard_map/all_gather | solution.py:134
  210.4 18.4 while.56
  247.2 96.7 %all-gather.16.cloned.1.call-done = bf16[1024,3072]{1,0:T(8,128)(2,1)} async-done(((bf16[128,3072]{1,0:T(8,128)(2,1)}), bf16[1024,3072]{1,0:T(8,128)(2,1)}) %all-gather.16.cloned.1.call-update) | async-done | bytes 6291472 | tf_op jit(solution)/shard_map/all_gather | solution.py:136
  376.3 20.9 %all-gather.20.cloned.1.call-done = bf16[1024,1024]{1,0:T(8,128)(2,1)} async-done(((bf16[256,1024]{1,0:T(8,128)(2,1)}), bf16[1024,1024]{1,0:T(8,128)(2,1)}) %all-gather.20.cloned.1.call-update) | async-done | bytes 2097168 | tf_op jit(solution)/shard_map/all_gather | solution.py:170
  402.0 22.9 %while.57 = (s32[]{:T(128)}, bf16[4,4,256,64]{2,3,1,0:T(8,128)(2,1)}, f32[4,4,256,1]{2,1,3,0:T(4,128)S(1)}, f32[4,4,256,1]{2,1,3,0:T(4,128)S(1)}, bf16[4,4,256,6...) while((s32[]{:T(128)}, ...), condition=%wide.region_12.13_spmd, body=%wide.region_9.12_spmd.sunk | while | flops 277870592 | bytes 18258072 | solution.py:67
  425.0 22.7 %all-gather.22.cloned.1.call-done = bf16[1024,1024]{1,0:T(8,128)(2,1)} async-done(((bf16[128,1024]{1,0:T(8,128)(2,1)}), bf16[1024,1024]{1,0:T(8,128)(2,1)}) %all-gather.22.cloned.1.call-update) | async-done | bytes 2097168 | tf_op jit(solution)/shard_map/all_gather | solution.py:137
  451.5 121.8 %all-gather.24.cloned.1.call-done = bf16[1024,4096]{1,0:T(8,128)(2,1)} async-done(((bf16[128,4096]{1,0:T(8,128)(2,1)}), bf16[1024,4096]{1,0:T(8,128)(2,1)}) %all-gather.24.cloned.1.call-update) | async-done | bytes 8388624 | tf_op jit(solution)/shard_map/all_gather | solution.py:138
  581.4 117.2 %all-gather.26.cloned.1.call-done = bf16[4096,1024]{1,0:T(8,128)(2,1)} async-done(((bf16[512,1024]{1,0:T(8,128)(2,1)}), bf16[4096,1024]{1,0:T(8,128)(2,1)}) %all-gather.26.cloned.1.call-update) | async-done | bytes 8388624 | tf_op jit(solution)/shard_map/all_gather | solution.py:139
  718.0 39.8 %while.58 = (s32[]{:T(128)}, bf16[4,4,256,64]{2,3,1,0:T(8,128)(2,1)}, f32[4,4,1024,64]{2,3,1,0:T(8,128)}, f32[4,4,1024,64]{2,3,1,0:T(8,128)}, bf16[4,4,256,64]{2...) while((s32[]{:T(128)}, ...), condition=%wide.region_19.20_spmd, body=%wide.region_17.19_spmd.sunk | while | flops 680852480 | bytes 48534732 | solution.py:102
  758.5 43.5 %reduce-scatter.14.cloned.1.call-done = f32[256,1024]{0,1:T(8,128)} async-done(((f32[1024,1024]{0,1:T(8,128)}), f32[256,1024]{0,1:T(8,128)}) %reduce-scatter.14.cloned.1.call-update) | async-done | bytes 1048592 | tf_op jit(solution)/shard_map/reduce_scatter | solution.py:197
  803.2 45.6 %reduce-scatter.12.cloned.1.call-done = f32[256,1024]{0,1:T(8,128)} async-done(((f32[1024,1024]{0,1:T(8,128)}), f32[256,1024]{0,1:T(8,128)}) %reduce-scatter.12.cloned.1.call-update) | async-done | bytes 1048592 | tf_op jit(solution)/shard_map/reduce_scatter | solution.py:196
  862.2 40.3 %while.59 = (s32[]{:T(128)}, bf16[4,4,256,64]{2,3,1,0:T(8,128)(2,1)}, bf16[4,4,1025,64]{2,3,1,0:T(8,128)(2,1)}, bf16[4,4,1025,64]{2,3,1,0:T(8,128)(2,1)}, pred[1...) while((s32[]{:T(128)}, ...), condition=%wide.region_26.27_spmd, body=%wide.region_24.26_spmd.sunk | while | flops 682566912 | bytes 82707776 | solution.py:102
  935.8 35.5 %reduce-scatter.18.cloned.1.call-done = bf16[1025,256]{0,1:T(8,128)(2,1)} async-done(((bf16[1025,1024]{0,1:T(8,128)(2,1)}), bf16[1025,256]{0,1:T(8,128)(2,1)}) %reduce-scatter.18.cloned.1.call-update) | async-done | bytes 524816 | tf_op jit(solution)/shard_map/reduce_scatter | solution.py:211
  993.8 46.3 %reduce-scatter.28.cloned.1.call-done = bf16[128,1024]{1,0:T(8,128)(2,1)} async-done(((bf16[1024,1024]{1,0:T(8,128)(2,1)}), bf16[128,1024]{1,0:T(8,128)(2,1)}) %reduce-scatter.28.cloned.1.call-update) | async-done | bytes 262160 | tf_op jit(solution)/shard_map/reduce_scatter | solution.py:277
  1040.1 71.4 %reduce-scatter.16.cloned.1.call-done = bf16[128,1024]{1,0:T(8,128)(2,1)} async-done(((bf16[1024,1024]{1,0:T(8,128)(2,1)}), bf16[128,1024]{1,0:T(8,128)(2,1)}) %reduce-scatter.16.cloned.1.call-update) | async-done | bytes 262160 | tf_op jit(solution)/shard_map/reduce_scatter | solution.py:265
  1111.5 71.1 %reduce-scatter.24.cloned.1.call-done = bf16[128,1024]{1,0:T(8,128)(2,1)} async-done(((bf16[1024,1024]{1,0:T(8,128)(2,1)}), bf16[128,1024]{1,0:T(8,128)(2,1)}) %reduce-scatter.24.cloned.1.call-update) | async-done | bytes 262160 | tf_op jit(solution)/shard_map/reduce_scatter | solution.py:271
  1182.6 153.6 %reduce-scatter.30.cloned.1.call-done = bf16[128,4096]{1,0:T(8,128)(2,1)} async-done(((bf16[1024,4096]{1,0:T(8,128)(2,1)}), bf16[128,4096]{1,0:T(8,128)(2,1)}) %reduce-scatter.30.cloned.1.call-update) | async-done | bytes 1048592 | tf_op jit(solution)/shard_map/reduce_scatter | solution.py:280
  1336.2 151.7 %reduce-scatter.32.cloned.1.call-done = bf16[512,1024]{1,0:T(8,128)(2,1)} async-done(((bf16[4096,1024]{1,0:T(8,128)(2,1)}), bf16[512,1024]{1,0:T(8,128)(2,1)}) %reduce-scatter.32.cloned.1.call-update) | async-done | bytes 1048592 | tf_op jit(solution)/shard_map/reduce_scatter | solution.py:283
  1487.9 77.6 %reduce-scatter.22.cloned.1.call-done = bf16[96,2048]{1,0:T(8,128)(2,1)} async-done(((bf16[768,2048]{1,0:T(8,128)(2,1)}), bf16[96,2048]{1,0:T(8,128)(2,1)}) %reduce-scatter.22.cloned.1.call-update) | async-done | bytes 393232 | tf_op jit(solution)/shard_map/reduce_scatter | solution.py:268
  1565.5 121.8 %reduce-scatter.26.cloned.1.call-done = bf16[128,3072]{1,0:T(8,128)(2,1)} async-done(((bf16[1024,3072]{1,0:T(8,128)(2,1)}), bf16[128,3072]{1,0:T(8,128)(2,1)}) %reduce-scatter.26.cloned.1.call-update) | async-done | bytes 786448 | tf_op jit(solution)/shard_map/reduce_scatter | solution.py:274
  1697.0 119.3 %all-reduce.7.cloned.1.call-done = f32[8,6144]{1,0:T(8,128)} async-done(((f32[8,6144]{1,0:T(8,128)}), f32[8,6144]{1,0:T(8,128)}) %all-reduce.7.cloned.1.call-update) | async-done | bytes 196624 | tf_op jit(solution)/shard_map/psum | solution.py:247
  1820.3 85.2 %all-reduce.9.cloned.1.call-done = (bf16[128,1024]{1,0:T(8,128)(2,1)}, bf16[96,2048]{1,0:T(8,128)(2,1)}, bf16[128,1024]{1,0:T(8,128)(2,1)}, bf16[128,3072]{1,0:T...) async-done(((bf16[128,1024]{1,0:T(8,128)(2,1)}, bf16[96,2048]{1,0:T(8,128)(2,1)}, bf16[128,1024]{1,0:T(8,128)(2,1)}, ...) | async-done | bytes 4063248 | tf_op jit(solution)/shard_map/psum | solution.py:288
  (443 shorter events, 330.5 us)
Async XLA Ops:
  7.2 72.9 %all-reduce.5.cloned.1.call-start = ((), (), s32[]{:S(2)}) async-start(), calls=%async_computation.11 | async-start | bytes 393216 | tf_op jit(solution)/shard_map/psum | solution.py:142
  9.8 122.9 %all-gather.10.cloned.1.call-start = ((), (), s32[]{:S(2)}) async-start(), calls=%async_computation.12 | async-start | bytes 2359296 | tf_op jit(solution)/shard_map/all_gather | solution.py:133
  10.6 183.4 %all-gather.12.cloned.1.call-start = ((), (), s32[]{:S(2)}) async-start(), calls=%async_computation.13 | async-start | bytes 3538944 | tf_op jit(solution)/shard_map/all_gather | solution.py:134
  11.3 232.9 %all-gather.14.cloned.1.call-start = ((), (), s32[]{:S(2)}) async-start(), calls=%async_computation.14 | async-start | bytes 2359296 | tf_op jit(solution)/shard_map/all_gather | solution.py:135
  11.9 332.0 %all-gather.16.cloned.1.call-start = ((), (), s32[]{:S(2)}) async-start(), calls=%async_computation.15 | async-start | bytes 7077888 | tf_op jit(solution)/shard_map/all_gather | solution.py:136
  12.5 359.9 %all-gather.18.cloned.1.call-start = ((), (), s32[]{:S(2)}) async-start(), calls=%async_computation.16 | async-start | bytes 2621440 | tf_op jit(solution)/shard_map/all_gather | solution.py:169
  349.8 47.5 %all-gather.20.cloned.1.call-start = ((), (), s32[]{:S(2)}) async-start(), calls=%async_computation.17 | async-start | bytes 2621440 | tf_op jit(solution)/shard_map/all_gather | solution.py:170
  350.5 97.1 %all-gather.22.cloned.1.call-start = ((), (), s32[]{:S(2)}) async-start(), calls=%async_computation.18 | async-start | bytes 2359296 | tf_op jit(solution)/shard_map/all_gather | solution.py:137
  351.3 222.0 %all-gather.24.cloned.1.call-start = ((), (), s32[]{:S(2)}) async-start(), calls=%async_computation.19 | async-start | bytes 9437184 | tf_op jit(solution)/shard_map/all_gather | solution.py:138
  352.0 346.6 %all-gather.26.cloned.1.call-start = ((), (), s32[]{:S(2)}) async-start(), calls=%async_computation.20 | async-start | bytes 9437184 | tf_op jit(solution)/shard_map/all_gather | solution.py:139
  352.6 449.4 %reduce-scatter.14.cloned.1.call-start = ((), (), s32[]{:S(2)}) async-start(), calls=%async_computation.22 | async-start | bytes 5242880 | tf_op jit(solution)/shard_map/reduce_scatter | solution.py:197
  757.8 91.1 %reduce-scatter.12.cloned.1.call-start = ((), (), s32[]{:S(2)}) async-start(), calls=%async_computation.21 | async-start | bytes 5242880 | tf_op jit(solution)/shard_map/reduce_scatter | solution.py:196
  758.4 177.4 %reduce-scatter.20.cloned.1.call-start = ((), (), s32[]{:S(2)}) async-start(), calls=%async_computation.26 | async-start | bytes 2949120 | tf_op jit(solution)/shard_map/reduce_scatter | solution.py:214
  902.7 68.6 %reduce-scatter.18.cloned.1.call-start = ((), (), s32[]{:S(2)}) async-start(), calls=%async_computation.25 | async-start | bytes 2949120 | tf_op jit(solution)/shard_map/reduce_scatter | solution.py:211
  903.2 136.9 %reduce-scatter.28.cloned.1.call-start = ((), (), s32[]{:S(2)}) async-start(), calls=%async_computation.30 | async-start | bytes 2359296 | tf_op jit(solution)/shard_map/reduce_scatter | solution.py:277
  906.6 204.9 %reduce-scatter.16.cloned.1.call-start = ((), (), s32[]{:S(2)}) async-start(), calls=%async_computation.24 | async-start | bytes 2359296 | tf_op jit(solution)/shard_map/reduce_scatter | solution.py:265
  910.2 272.4 %reduce-scatter.24.cloned.1.call-start = ((), (), s32[]{:S(2)}) async-start(), calls=%async_computation.28 | async-start | bytes 2359296 | tf_op jit(solution)/shard_map/reduce_scatter | solution.py:271
  913.9 422.3 %reduce-scatter.30.cloned.1.call-start = ((), (), s32[]{:S(2)}) async-start(), calls=%async_computation.31 | async-start | bytes 9437184 | tf_op jit(solution)/shard_map/reduce_scatter | solution.py:280
  921.7 566.2 %reduce-scatter.32.cloned.1.call-start = ((), (), s32[]{:S(2)}) async-start(), calls=%async_computation.32 | async-start | bytes 9437184 | tf_op jit(solution)/shard_map/reduce_scatter | solution.py:283
  930.4 635.1 %reduce-scatter.22.cloned.1.call-start = ((), (), s32[]{:S(2)}) async-start(), calls=%async_computation.27 | async-start | bytes 3538944 | tf_op jit(solution)/shard_map/reduce_scatter | solution.py:268
  981.2 706.0 %reduce-scatter.26.cloned.1.call-start = ((), (), s32[]{:S(2)}) async-start(), calls=%async_computation.29 | async-start | bytes 7077888 | tf_op jit(solution)/shard_map/reduce_scatter | solution.py:274
  987.5 699.8 %copy-start.5 = (f32[256,1024]{1,0:T(8,128)S(1)}, f32[256,1024]{1,0:T(8,128)}, u32[]{:S(2)}) copy-start(f32[256,1024]{1,0:T(8,128)} %copy-done.3) | copy-start | bytes 3145732
  987.5 828.8 %all-reduce.7.cloned.1.call-start = ((), (), s32[]{:S(2)}) async-start(), calls=%async_computation.23 | async-start | bytes 393216 | tf_op jit(solution)/shard_map/psum | solution.py:247
  993.8 911.7 %all-reduce.9.cloned.1.call-start = ((), (), s32[]{:S(2)}) async-start(), calls=%async_computation.33 | async-start | bytes 8126464 | tf_op jit(solution)/shard_map/psum | solution.py:288
  (106 other events, 4646.1 us)
Sparse Core Ops, SparseCore 0:
  11.9 68.1 all-reduce.4
  82.5 50.2 all-gather.9
  135.1 58.8 all-gather.11
  196.2 47.9 all-gather.13
  246.5 97.2 all-gather.15
  349.9 22.4 all-gather.17
  374.6 22.5 all-gather.19
  399.6 48.0 all-gather.21
  450.0 123.1 all-gather.23
  575.4 123.1 all-gather.25
  757.9 43.9 reduce-scatter.13
  804.3 44.4 reduce-scatter.11
  902.7 33.0 reduce-scatter.19
  938.2 33.0 reduce-scatter.17
  975.1 64.9 reduce-scatter.27
  1044.5 66.9 reduce-scatter.15
  1115.8 66.7 reduce-scatter.23
  1186.5 149.6 reduce-scatter.29
  1339.8 147.9 reduce-scatter.31
  1492.3 73.1 reduce-scatter.21
  1569.5 117.7 reduce-scatter.25
  1694.3 121.9 all-reduce.6
  1819.4 86.0 all-reduce.8
where the time goes:
time: 1940 us; the launch traced here: 1920 us
  waiting for transfers between devices  1620 us (84%)
  matrix products  194 us (10%)
  local copies, waits for them, and re-layouts  57.5 us (3%)
  other arithmetic  31.7 us (2%)
    reduce_scatter x1, waiting for transfers between devices, local(): lax.psum_scatter(terms[5].astype(jnp.bfloat16), 'batch', scatter_dimensio...  154 us
    reduce_scatter x1, waiting for transfers between devices, local(): lax.psum_scatter(terms[6].astype(jnp.bfloat16), 'batch', scatter_dimensio...  152 us
    reduce_scatter x1, waiting for transfers between devices, local(): lax.psum_scatter(terms[3].astype(jnp.bfloat16), 'batch', scatter_dimensio...  122 us
    all_gather x1, waiting for transfers between devices, local(): lax.all_gather(mlp_in, 'batch', axis=0, tiled=True)  122 us
    psum x1, waiting for transfers between devices, local(): grad_table = lax.psum(grad_table, ('batch', 'seq'))  119 us
    all_gather x1, waiting for transfers between devices, local(): lax.all_gather(mlp_out, 'batch', axis=0, tiled=True)  117 us
    all_gather x1, waiting for transfers between devices, local(): lax.all_gather(qkv_self, 'batch', axis=0, tiled=True)  96.7 us
    psum x1, waiting for transfers between devices, local(): lax.psum(shares[0].astype(jnp.bfloat16), 'seq').astype(jnp.float32)  85.2 us
  transfers between devices with their start and end apart: 23, of which 23 were waited for; matrix products, arithmetic and copies ran while one was open for 8% of the time, Pallas kernels for 0%

commit v1 on v0

--- a/solution.py
+++ b/solution.py
@@ -1,6 +1,10 @@
+import functools
+
 import jax
 import jax.numpy as jnp
 from jax import lax
+from jax.experimental import pallas as pl
+from jax.experimental.pallas import tpu as pltpu
 from jax.sharding import PartitionSpec as P
 
 HEADS = 16
@@ -10,6 +14,7 @@
 epsilon = 1e-06
 group_heads = 4
 highest = lax.Precision.HIGHEST
+LIMIT = 64 * 1024 * 1024 - 64 * 1024
 
 
 def modulated_norm(values, shift, scale):
@@ -307,9 +312,1182 @@
     )
 
 
+bf16 = jnp.bfloat16
+f32 = jnp.float32
+MESH = pl.DeviceIdType.MESH
+BELOW = -3.0e38
+
+
+def nn(a, b):
+    return jnp.dot(a, b, preferred_element_type=f32)
+
+
+def nt(a, b):
+    return lax.dot_general(a, b, (((1,), (1,)), ((), ())), preferred_element_type=f32)
+
+
+def tn(a, b):
+    return lax.dot_general(a, b, (((0,), (0,)), ((), ())), preferred_element_type=f32)
+
+
+def one_head(pair, side):
+    lane = lax.broadcasted_iota(jnp.int32, pair.shape, 1)
+    return jnp.where(lane // HEAD_DIM == side, pair, jnp.zeros_like(pair))
+
+
+def two_heads(first, second):
+    lane = lax.broadcasted_iota(jnp.int32, first.shape, 1)
+    return jnp.where(lane < HEAD_DIM, first, second)
+
+
+def softmax_rows(scores, mask):
+    if mask is not None:
+        scores = jnp.where(mask[0:1, :] > 0.5, scores, mask[1:2, :])
+    expo = jnp.exp(scores - jnp.max(scores, axis=-1, keepdims=True))
+    return expo * (1.0 / jnp.sum(expo, axis=-1, keepdims=True))
+
+
+def norm_stats(rows):
+    center = rows - jnp.mean(rows, axis=-1, keepdims=True)
+    inverse = lax.rsqrt(jnp.mean(center * center, axis=-1, keepdims=True) + epsilon)
+    return center * inverse, inverse
+
+
+def norm_forward(rows, shift, scale):
+    return norm_stats(rows)[0] * (1.0 + scale) + shift
+
+
+def norm_backward(rows, scale, grad):
+    normed, inverse = norm_stats(rows)
+    inner = grad * (1.0 + scale)
+    mean_inner = jnp.mean(inner, axis=-1, keepdims=True)
+    mean_cross = jnp.mean(inner * normed, axis=-1, keepdims=True)
+    grad_rows = inverse * (inner - mean_inner - normed * mean_cross)
+    return (
+        grad_rows,
+        jnp.sum(grad, axis=0, keepdims=True),
+        jnp.sum(grad * normed, axis=0, keepdims=True),
+    )
+
+
+Q, KV, OC, QKV, OS, UP, DOWN, CAMERA, TABLE, TOKENS, OWN, IMAGE, COTANGENT = range(13)
+
+
+class Sizes:
+    def __init__(self, mesh_shape, inputs):
+        self.batch, self.seq = mesh_shape["batch"], mesh_shape["seq"]
+        self.own, self.width = inputs[0].shape[1:]
+        self.image_rows, self.image_width = inputs[2].shape[1:]
+        self.chunks = 4
+        self.part = self.own // self.chunks
+        self.rows = self.seq * self.part
+        self.tokens = self.seq * self.own
+        self.columns = self.width // self.seq
+        self.hidden = inputs[12].shape[1] // self.seq
+        self.keys = -(-self.image_rows // 128) * 128
+        self.whole_rows = self.image_rows // 16 * 16
+        self.block = self.width // self.batch
+        self.image_block = self.image_width // self.batch
+        self.weights = (
+            (self.block, self.columns),
+            (self.image_block, 2 * self.columns),
+            (self.block, self.width),
+            (self.block, 3 * self.columns),
+            (self.block, self.width),
+            (self.block, self.hidden),
+            (self.hidden // self.batch, self.width),
+        )
+
+
+class Refs:
+    def __init__(self, refs):
+        rest = iter(refs)
+        self.tokens = next(rest)
+        self.cotangent = next(rest)
+        self.image = next(rest)
+        self.tail = next(rest)
+        self.mask = next(rest)
+        self.camera = next(rest)
+        self.modulation = next(rest)
+        self.q_cross = next(rest)
+        self.kv_image = next(rest)
+        self.out_cross = next(rest)
+        self.qkv_self = next(rest)
+        self.out_self = next(rest)
+        self.mlp_in = next(rest)
+        self.mlp_out = next(rest)
+        self.output = next(rest)
+        self.grad_tokens = next(rest)
+        self.table = next(rest)
+        self.gout = [next(rest) for _ in range(7)]
+        self.weights = [next(rest) for _ in range(7)]
+        self.firsts = [next(rest) for _ in range(7)]
+        self.seconds = [next(rest) for _ in range(7)]
+        self.buf_a = next(rest)
+        self.buf_b = next(rest)
+        self.buf_h2 = next(rest)
+        self.buf_b2 = next(rest)
+        self.part_main = next(rest)
+        self.core_main = next(rest)
+        self.send_main = next(rest)
+        self.line_main = next(rest)
+        self.part_side = next(rest)
+        self.core_side = next(rest)
+        self.send_side = next(rest)
+        self.line_side = next(rest)
+        self.image_all = next(rest)
+        self.mask_all = next(rest)
+        self.camera_own = next(rest)
+        self.mods_all = next(rest)
+        self.mods = next(rest)
+        self.sums = next(rest)
+        self.sums_seq = next(rest)
+        self.normed1 = next(rest)
+        self.query1 = next(rest)
+        self.key1 = next(rest)
+        self.value1 = next(rest)
+        self.att1 = next(rest)
+        self.packed2 = next(rest)
+        self.att2 = next(rest)
+        self.hidden = next(rest)
+        self.grad_up = next(rest)
+        self.grad_key = next(rest)
+        self.grad_value = next(rest)
+        self.x0 = next(rest)
+        self.x1 = next(rest)
+        self.x2 = next(rest)
+        self.grads_a = next(rest)
+        self.grads_b = next(rest)
+        self.grads_c = next(rest)
+        self.sem_load = next(rest)
+        self.sem_wz_s = next(rest)
+        self.sem_wz_r = next(rest)
+        self.sem_wx_s = next(rest)
+        self.sem_wx_r = next(rest)
+        self.sem_gx_s = next(rest)
+        self.sem_gx_r = next(rest)
+        self.sem_gz_s = next(rest)
+        self.sem_gz_r = next(rest)
+        self.sem_gs_s = next(rest)
+        self.sem_gs_r = next(rest)
+        self.sem_in_s = next(rest)
+        self.sem_in_r = next(rest)
+        self.sem_ag_s = next(rest)
+        self.sem_ag_r = next(rest)
+        self.sem_rs_s = next(rest)
+        self.sem_rs_r = next(rest)
+        self.sem_m_s = next(rest)
+        self.sem_m_r = next(rest)
+        self.sem_d_s = next(rest)
+        self.sem_d_r = next(rest)
+        self.sem_t_s = next(rest)
+        self.sem_t_r = next(rest)
+        self.sem_out = next(rest)
+
+
+def whole_layer(z, *refs):
+    r = Refs(refs)
+    W, FIRST, SECOND, GOUT = r.weights, r.firsts, r.seconds, r.gout
+    n, S, B = z.chunks, z.seq, z.batch
+    part, rows, D, C = z.part, z.rows, z.width, z.columns
+    Z = B // 2
+    b = lax.axis_index("batch")
+    s = lax.axis_index("seq")
+    zz = b // 2
+    x = lax.rem(b, 2)
+    y = s // 2
+    c = lax.rem(s, 2)
+    other_x = 1 - x
+    other_c = 1 - c
+    other_y = 1 - y
+    x_peer = (2 * zz + other_x, s)
+    core_peer = (b, 2 * y + other_c)
+    line_peer = (b, 2 * other_y + c)
+    line_slot = 2 * other_y + c
+    core_slot = 2 * y + other_c
+    far_slot = 2 * other_y + other_c
+
+    def z_of(j):
+        return lax.rem(zz + j, Z)
+
+    def remote(src, dst, send, recv, device):
+        return pltpu.make_async_remote_copy(
+            src_ref=src,
+            dst_ref=dst,
+            send_sem=send,
+            recv_sem=recv,
+            device_id=device,
+            device_id_type=MESH,
+        )
+
+    def arrived(dst, send, recv, device):
+        remote(dst, dst, send, recv, device).wait_recv()
+
+    barrier = pltpu.get_barrier_semaphore()
+    for j in range(1, B):
+        pl.semaphore_signal(barrier, inc=1, device_id=(lax.rem(b + j, B), s), device_id_type=MESH)
+    for j in range(1, S):
+        pl.semaphore_signal(barrier, inc=1, device_id=(b, lax.rem(s + j, S)), device_id_type=MESH)
+
+    loads = {}
+
+    def load(key, src, dst, when=None):
+        count = sum(len(copies) for copies in loads.values())
+        copy = pltpu.make_async_copy(src, dst, r.sem_load.at[count])
+        loads.setdefault(key, []).append(copy)
+        if when is None:
+            copy.start()
+        else:
+            pl.when(when)(copy.start)
+
+    def col(index, width):
+        return pl.ds(pl.multiple_of(index * width, 128), width)
+
+    load(CAMERA, r.camera, r.camera_own)
+    for k in range(6):
+        load(
+            TABLE,
+            r.modulation.at[:, pl.ds(k * D, D)],
+            r.hidden.at[pl.ds(k * z.block, z.block)],
+        )
+    for j in range(2):
+        load(
+            KV,
+            r.kv_image.at[:, pl.ds(pl.multiple_of(j * D + s * C, 128), C)],
+            W[KV].at[b, :, pl.ds(j * C, C)],
+        )
+    load(TOKENS, r.tokens, r.buf_a.at[:, s])
+    load(Q, r.q_cross.at[:, col(s, C)], W[Q].at[b])
+    load(IMAGE, r.image.at[pl.ds(0, z.whole_rows)], r.image_all.at[pl.ds(0, z.whole_rows)])
+    load(IMAGE, r.tail, r.image_all.at[pl.ds(z.whole_rows, z.keys - z.whole_rows)])
+    load(IMAGE, r.mask, r.mask_all)
+    load(OWN, r.tokens, r.x0)
+    load(OC, r.out_cross, W[OC].at[x], zz == s)
+    for j in range(3):
+        load(
+            QKV,
+            r.qkv_self.at[:, pl.ds(pl.multiple_of(j * D + s * C, 128), C)],
+            W[QKV].at[b, :, pl.ds(j * C, C)],
+        )
+    load(OS, r.out_self, W[OS].at[x], zz == s)
+    wide = z.hidden // B
+    for j in range(B):
+        load(
+            UP,
+            r.mlp_in.at[:, pl.ds(pl.multiple_of(j * (z.hidden * S // B) + s * wide, 128), wide)],
+            W[UP].at[b, :, pl.ds(j * wide, wide)],
+        )
+    load(DOWN, r.mlp_out.at[pl.ds(pl.multiple_of(s * wide, 128), wide), :], W[DOWN].at[b])
+    load(COTANGENT, r.cotangent, r.buf_b.at[:, s])
+
+    pl.semaphore_wait(barrier, B - 1 + S - 1)
+
+    by_rows = (OC, OS)
+    def loaded(key):
+        for copy in loads[key]:
+            copy.wait()
+
+    def z_send(w, j):
+        slot = x if w in by_rows else b
+        mark = 0 if w in by_rows else zz
+        return remote(
+            W[w].at[slot],
+            W[w].at[slot],
+            r.sem_wz_s.at[w, j - 1],
+            r.sem_wz_r.at[w, mark],
+            (2 * z_of(j) + x, s),
+        )
+
+    def x_send(w, from_z):
+        slot = x if w in by_rows else 2 * from_z + x
+        mark = 0 if w in by_rows else from_z
+        return remote(
+            W[w].at[slot],
+            W[w].at[slot],
+            r.sem_wx_s.at[w, mark],
+            r.sem_wx_r.at[w, mark],
+            x_peer,
+        )
+
+    def weight_start(w):
+        def go():
+            loaded(w)
+            for j in range(1, Z):
+                z_send(w, j).start()
+            x_send(w, zz).start()
+
+        if w in by_rows:
+            pl.when(zz == s)(go)
+        else:
+            go()
+
+    def weight_pass(w):
+        if w in by_rows:
+
+            @pl.when(zz != s)
+            def _():
+                arrived(
+                    W[w].at[x], r.sem_wz_s.at[w, 0], r.sem_wz_r.at[w, 0], (2 * s + x, s)
+                )
+                x_send(w, zz).start()
+
+        else:
+            for j in range(1, Z):
+                from_z = z_of(j)
+                arrived(
+                    W[w].at[2 * from_z + x],
+                    r.sem_wz_s.at[w, 0],
+                    r.sem_wz_r.at[w, from_z],
+                    (2 * from_z + x, s),
+                )
+                x_send(w, from_z).start()
+
+    def weight_wait(w):
+        for from_z in [0] if w in by_rows else range(Z):
+            slot = other_x if w in by_rows else 2 * from_z + other_x
+            arrived(W[w].at[slot], r.sem_wx_s.at[w, 0], r.sem_wx_r.at[w, from_z], x_peer)
+
+    def weight_drain(w):
+        if w in by_rows:
+
+            @pl.when(zz == s)
+            def _():
+                for j in range(1, Z):
+                    z_send(w, j).wait_send()
+
+            x_send(w, zz).wait_send()
+        else:
+            for j in range(1, Z):
+                z_send(w, j).wait_send()
+            for j in range(Z):
+                x_send(w, z_of(j)).wait_send()
+
+    def give(buf, i, k):
+        slot, peer = [(s, core_peer), (s, line_peer), (line_slot, core_peer)][k]
+        return remote(
+            buf.at[i, slot], buf.at[i, slot], r.sem_ag_s.at[i, k], r.sem_ag_r.at[i, k], peer
+        )
+
+    def gather_start(buf, i):
+        give(buf, i, 1).start()
+        give(buf, i, 0).start()
+
+    def gather_pass(buf, i):
+        arrived(buf.at[i, line_slot], r.sem_ag_s.at[i, 1], r.sem_ag_r.at[i, 1], line_peer)
+        give(buf, i, 2).start()
+
+    def gather_wait(buf, i):
+        arrived(buf.at[i, core_slot], r.sem_ag_s.at[i, 0], r.sem_ag_r.at[i, 0], core_peer)
+        arrived(buf.at[i, far_slot], r.sem_ag_s.at[i, 2], r.sem_ag_r.at[i, 2], core_peer)
+        for k in range(3):
+            give(buf, i, k).wait_send()
+
+    def give_input(buf, m, k):
+        slot, peer = [(s, core_peer), (s, line_peer), (line_slot, core_peer)][k]
+        return remote(
+            buf.at[:, slot], buf.at[:, slot], r.sem_in_s.at[m, k], r.sem_in_r.at[m, k], peer
+        )
+
+    def input_start(buf, m):
+        give_input(buf, m, 1).start()
+        give_input(buf, m, 0).start()
+
+    def input_pass(buf, m):
+        arrived(buf.at[:, line_slot], r.sem_in_s.at[m, 1], r.sem_in_r.at[m, 1], line_peer)
+        give_input(buf, m, 2).start()
+
+    def input_wait(buf, m):
+        arrived(buf.at[:, core_slot], r.sem_in_s.at[m, 0], r.sem_in_r.at[m, 0], core_peer)
+        arrived(buf.at[:, far_slot], r.sem_in_s.at[m, 2], r.sem_in_r.at[m, 2], core_peer)
+        for k in range(3):
+            give_input(buf, m, k).wait_send()
+
+    lanes = (
+        (r.part_main, r.core_main, r.send_main, r.line_main),
+        (r.part_side, r.core_side, r.send_side, r.line_side),
+    )
+
+    def sum_core(lane, i):
+        mine, core, _, _ = lanes[lane]
+        return remote(
+            mine.at[i, :, other_c],
+            core.at[i],
+            r.sem_rs_s.at[lane, i, 0],
+            r.sem_rs_r.at[lane, i, 0],
+            core_peer,
+        )
+
+    def sum_line(lane, i):
+        _, _, send, line = lanes[lane]
+        return remote(
+            send.at[i],
+            line.at[i],
+            r.sem_rs_s.at[lane, i, 1],
+            r.sem_rs_r.at[lane, i, 1],
+            line_peer,
+        )
+
+    def sum_start(lane, i, value):
+        lanes[lane][0][i] = value.astype(bf16).reshape(2, 2, part, D)
+        sum_core(lane, i).start()
+
+    def sum_pass(lane, i):
+        mine, core, send, _ = lanes[lane]
+        sum_core(lane, i).wait_recv()
+        send[i] = (mine[i, other_y, c].astype(f32) + core[i, other_y].astype(f32)).astype(bf16)
+        sum_line(lane, i).start()
+
+    def sum_end(lane, i):
+        mine, core, _, line = lanes[lane]
+        sum_line(lane, i).wait_recv()
+        total = mine[i, y, c].astype(f32) + core[i, y].astype(f32) + line[i].astype(f32)
+        sum_core(lane, i).wait_send()
+        sum_line(lane, i).wait_send()
+        return total
+
+    def grad_place(w):
+        return {
+            Q: r.grads_b.at[:, :, :, pl.ds(0, C)],
+            KV: r.grads_b.at[:, :, pl.ds(0, z.image_block), pl.ds(C, 2 * C)],
+            OC: r.grads_c.at[0],
+            QKV: r.grads_a.at[:, :, :, pl.ds(0, 3 * C)],
+            OS: r.grads_c.at[1],
+            UP: r.grads_a,
+            DOWN: r.grads_b,
+        }[w]
+
+    def grad_x(w):
+        place = grad_place(w)
+        src = place.at[other_x] if w in by_rows else place.at[:, other_x]
+        return remote(src, FIRST[w], r.sem_gx_s.at[w], r.sem_gx_r.at[w], x_peer)
+
+    def grad_z(w, j):
+        if w in by_rows:
+            return remote(
+                FIRST[w],
+                SECOND[w].at[lax.rem(zz - s + Z, Z) - 1],
+                r.sem_gz_s.at[w, 0],
+                r.sem_gz_r.at[w, zz],
+                (2 * s + x, s),
+            )
+        return remote(
+            FIRST[w].at[z_of(j)],
+            SECOND[w].at[Z - j - 1],
+            r.sem_gz_s.at[w, j - 1],
+            r.sem_gz_r.at[w, zz],
+            (2 * z_of(j) + x, s),
+        )
+
+    def grad_s(w, j):
+        src = FIRST[w] if w in by_rows else FIRST[w].at[zz]
+        dst = GOUT[w] if w in by_rows else GOUT[w].at[s]
+        mark = 0 if w in by_rows else s
+        return remote(
+            src,
+            dst,
+            r.sem_gs_s.at[w, j - 1],
+            r.sem_gs_r.at[w, mark],
+            (b, lax.rem(s + j, S)),
+        )
+
+    def grad_own(w):
+        src = FIRST[w] if w in by_rows else FIRST[w].at[zz]
+        dst = GOUT[w] if w in by_rows else GOUT[w].at[s]
+        return pltpu.make_async_copy(src, dst, r.sem_out.at[w])
+
+    def grad_start(w):
+        grad_x(w).start()
+
+    def grad_pass(w):
+        grad_x(w).wait_recv()
+        place = grad_place(w)
+        if w in by_rows:
+            FIRST[w][...] = (FIRST[w][...].astype(f32) + place[x].astype(f32)).astype(bf16)
+
+            @pl.when(zz != s)
+            def _():
+                grad_z(w, 0).start()
+
+        else:
+            for k in range(Z):
+                FIRST[w][k] = (FIRST[w][k].astype(f32) + place[k, x].astype(f32)).astype(bf16)
+            for j in range(1, Z):
+                grad_z(w, j).start()
+        grad_x(w).wait_send()
+
+    def grad_end(w):
+        if w in by_rows:
+
+            @pl.when(zz == s)
+            def _():
+                total = FIRST[w][...].astype(f32)
+                for j in range(1, Z):
+                    k = z_of(j)
+                    arrived(SECOND[w].at[j - 1], r.sem_gz_s.at[w, 0], r.sem_gz_r.at[w, k], (2 * k + x, s))
+                    total = total + SECOND[w][j - 1].astype(f32)
+                FIRST[w][...] = total.astype(bf16)
+                for j in range(1, S):
+                    grad_s(w, j).start()
+                grad_own(w).start()
+
+            @pl.when(zz != s)
+            def _():
+                grad_z(w, 0).wait_send()
+
+        else:
+            total = FIRST[w][zz].astype(f32)
+            for j in range(1, Z):
+                k = z_of(j)
+                arrived(SECOND[w].at[j - 1], r.sem_gz_s.at[w, 0], r.sem_gz_r.at[w, k], (2 * k + x, s))
+                total = total + SECOND[w][j - 1].astype(f32)
+            for j in range(1, Z):
+                grad_z(w, j).wait_send()
+            FIRST[w][zz] = total.astype(bf16)
+            for j in range(1, S):
+                grad_s(w, j).start()
+            grad_own(w).start()
+
+    def grad_drain(w):
+        if w in by_rows:
+
+            @pl.when(zz == s)
+            def _():
+                for j in range(1, S):
+                    grad_s(w, j).wait_send()
+                grad_own(w).wait()
+
+            @pl.when(zz != s)
+            def _():
+                arrived(GOUT[w], r.sem_gs_s.at[w, 0], r.sem_gs_r.at[w, 0], (b, zz))
+
+        else:
+            for j in range(1, S):
+                k = lax.rem(s + j, S)
+                arrived(GOUT[w].at[k], r.sem_gs_s.at[w, 0], r.sem_gs_r.at[w, k], (b, k))
+            for j in range(1, S):
+                grad_s(w, j).wait_send()
+            grad_own(w).wait()
+
+    def mods_send(j):
+        to = lax.rem(b + j, B)
+        return remote(
+            r.x2.at[0, pl.ds(pl.multiple_of(8 * to, 8), 8)],
+            r.mods_all.at[b],
+            r.sem_m_s.at[j - 1],
+            r.sem_m_r.at[b],
+            (to, s),
+        )
+
+    loaded(CAMERA)
+    loaded(TABLE)
+    camera = r.camera_own[...].astype(f32)
+    gate = (camera * jax.nn.sigmoid(camera)).astype(bf16)
+    for k in range(6):
+        term = nn(gate, r.hidden[k * z.block : (k + 1) * z.block, :])
+        for o in range(B):
+            r.x2[0, 8 * o + k : 8 * o + k + 1, :] = term[o : o + 1, :]
+    weight_start(KV)
+    loaded(TOKENS)
+    input_start(r.buf_a, 0)
+    for j in range(1, B):
+        mods_send(j).start()
+    weight_start(Q)
+    loaded(COTANGENT)
+    input_start(r.buf_b, 1)
+    weight_start(OC)
+    weight_start(QKV)
+    loaded(IMAGE)
+    loaded(OWN)
+
+    mods = r.x2[0, pl.ds(pl.multiple_of(8 * b, 8), 8)]
+    for j in range(1, B):
+        k = lax.rem(b + j, B)
+        arrived(r.mods_all.at[k], r.sem_m_s.at[0], r.sem_m_r.at[k], (k, s))
+        mods = mods + r.mods_all[k]
+    r.mods[...] = mods
+    for j in range(1, B):
+        mods_send(j).wait_send()
+
+    def mod(k):
+        return r.mods[k : k + 1, :]
+
+    weight_pass(KV)
+    input_pass(r.buf_a, 0)
+    weight_pass(Q)
+    weight_wait(KV)
+    scale_q = HEAD_DIM ** (-0.5)
+    step = z.keys // 3 if z.keys % 48 == 0 else z.keys
+
+    def project_image(k, _):
+        part_rows = pl.ds(pl.multiple_of(k * step, 16), step)
+        both = nn(r.image_all[part_rows, :], W[KV][...].reshape(z.image_width, 2 * C))
+        r.key1[part_rows, :] = both[:, :C].astype(bf16)
+        r.value1[part_rows, :] = both[:, C:].astype(bf16)
+        return 0
+
+    lax.fori_loop(0, z.keys // step, project_image, 0)
+    input_wait(r.buf_a, 0)
+    weight_wait(Q)
+
+    def chunk(i):
+        return pl.ds(pl.multiple_of(i * rows, rows), rows)
+
+    def project_query(i):
+        rows_in = r.buf_a[i].reshape(rows, D).astype(f32)
+        normed = norm_forward(rows_in, mod(0), mod(1)).astype(bf16)
+        r.normed1[chunk(i), :] = normed
+        query = nn(normed, W[Q][...].reshape(D, C)).astype(bf16)
+        r.query1[chunk(i), :] = (query * scale_q).astype(bf16)
+
+    def attend(i, query, key, value, att, mask):
+        for p in range(C // 128):
+            lane = slice(128 * p, 128 * p + 128)
+            pair = query(i, lane)
+            keys, values = key(lane), value(lane)
+            result = []
+            for side in range(2):
+                probs = softmax_rows(nt(one_head(pair, side), keys), mask).astype(bf16)
+                result.append(nn(probs, values))
+            att[chunk(i), lane] = two_heads(*result).astype(bf16)
+
+    def attend_back(i, query, key, value, grad, mask, grad_query):
+        query_t = query(i, slice(0, C)).T
+        grad_t = grad.T
+        for p in range(C // 128):
+            lane = slice(128 * p, 128 * p + 128)
+            pair, grad_pair = query(i, lane), grad[:, lane]
+            keys, values = key(lane), value(lane)
+            result = []
+            for side in range(2):
+                head = slice(128 * p + HEAD_DIM * side, 128 * p + HEAD_DIM * (side + 1))
+                probs = softmax_rows(nt(one_head(pair, side), keys), mask)
+                grad_probs = nt(one_head(grad_pair, side), values)
+                inner = jnp.sum(probs * grad_probs, axis=-1, keepdims=True)
+                scores = (probs * (grad_probs - inner)).astype(bf16)
+                count = keys.shape[0]
+                value_term = nn(grad_t[head, :], probs.astype(bf16))
+                key_term = nn(query_t[head, :], scores)
+                r.grad_value[head, :count] += value_term
+                r.grad_key[head, :count] += key_term
+                result.append(nn(scores, keys))
+            grad_query[chunk(i), lane] = (two_heads(*result) * scale_q).astype(bf16)
+
+    cross = (
+        lambda i, lane: r.query1[chunk(i), lane],
+        lambda lane: r.key1[:, lane],
+        lambda lane: r.value1[:, lane],
+    )
+
+    def plus(lane, offset):
+        return slice(lane.start + offset, lane.stop + offset)
+
+    own = (
+        lambda i, lane: r.packed2[chunk(i), lane],
+        lambda lane: r.packed2[:, plus(lane, C)],
+        lambda lane: r.packed2[:, plus(lane, 2 * C)],
+    )
+    mask_rows = r.mask_all
+
+    def pipeline(*stages):
+        last = max(offset for offset, _ in stages)
+
+        def body(step, _):
+            for offset, stage in stages:
+                i = step - offset
+
+                @pl.when((i >= 0) & (i < n))
+                def _():
+                    stage(i)
+
+            return 0
+
+        lax.fori_loop(0, n + last, body, 0)
+
+    def at(i, value, stage):
+        pl.when(i == value)(stage)
+
+    def weights_on(*steps):
+        def run():
+            for step, w in steps:
+                step(w)
+
+        return run
+
+    def cross_forward(i):
+        project_query(i)
+        attend(i, *cross, r.att1, mask_rows)
+        at(i, 0, weights_on((weight_start, OS), (weight_pass, OC), (weight_wait, OC)))
+        at(i, 1, weights_on((weight_start, UP)))
+        at(i, 2, weights_on((weight_pass, QKV), (weight_start, DOWN)))
+        at(i, 3, weights_on((weight_pass, OS)))
+        sum_start(0, i, nn(r.att1[chunk(i), :], W[OC][...].reshape(C, D)))
+
+    def after_cross(i):
+        total = r.x0[i].astype(f32) + sum_end(0, i)
+        r.x1[i] = total
+        r.buf_h2[i, s] = norm_forward(total, mod(2), mod(3)).astype(bf16)
+        gather_start(r.buf_h2, i)
+
+    def project_self(i):
+        at(i, 0, weights_on((weight_wait, QKV)))
+        gather_wait(r.buf_h2, i)
+        packed = nn(r.buf_h2[i].reshape(rows, D), W[QKV][...].reshape(D, 3 * C)).astype(bf16)
+        r.packed2[chunk(i), :C] = (packed[:, :C] * scale_q).astype(bf16)
+        r.packed2[chunk(i), C:] = packed[:, C:]
+
+    pipeline(
+        (0, cross_forward),
+        (1, lambda i: sum_pass(0, i)),
+        (2, after_cross),
+        (3, lambda i: gather_pass(r.buf_h2, i)),
+        (4, project_self),
+    )
+
+    weight_wait(OS)
+    input_pass(r.buf_b, 1)
+    input_wait(r.buf_b, 1)
+    r.sums[...] = jnp.zeros_like(r.sums)
+
+    def clear_keys():
+        r.grad_key[...] = jnp.zeros_like(r.grad_key)
+        r.grad_value[...] = jnp.zeros_like(r.grad_value)
+
+    clear_keys()
+
+    def output_copy(i):
+        return pltpu.make_async_copy(
+            r.part_side.at[i, 0, 0], r.output.at[i], r.sem_out.at[9 + i]
+        )
+
+    def self_forward(i):
+        attend(i, *own, r.att2, None)
+        at(i, 0, weights_on((weight_pass, UP)))
+        at(i, 2, weights_on((weight_pass, DOWN)))
+        sum_start(0, i, nn(r.att2[chunk(i), :], W[OS][...].reshape(C, D)))
+
+    def after_self(i):
+        total = r.x1[i] + sum_end(0, i)
+        r.x2[i] = total
+        r.buf_a[i, s] = norm_forward(total, mod(4), mod(5)).astype(bf16)
+        gather_start(r.buf_a, i)
+
+    def feed(i):
+        at(i, 0, weights_on((weight_wait, UP), (weight_wait, DOWN)))
+        gather_wait(r.buf_a, i)
+        rows_in = r.buf_a[i].reshape(rows, D)
+        grad_out = r.buf_b[i].reshape(rows, D)
+        up = W[UP]
+        down = W[DOWN]
+        forward = backward = None
+        pieces = 2
+        wide_piece = z.hidden // pieces
+        for k in range(pieces):
+            lane = slice(k * wide_piece, (k + 1) * wide_piece)
+            up_piece = up[:, :, lane].reshape(D, wide_piece)
+            down_piece = down[k * (B // pieces) : (k + 1) * (B // pieces)].reshape(wide_piece, D)
+            u = nn(rows_in, up_piece)
+            square = u * u
+            root = 0.7978845608028654
+            tanh = jnp.tanh(root * u * (1.0 + 0.044715 * square))
+            half = 0.5 * (1.0 + tanh)
+            hidden = (u * half).astype(bf16)
+            slope = half + 0.5 * u * (1.0 - tanh * tanh) * (root * (1.0 + 0.134145 * square))
+            grad_up = (nt(grad_out, down_piece) * slope).astype(bf16)
+            r.hidden[chunk(i), lane] = hidden
+            r.grad_up[chunk(i), lane] = grad_up
+            first = nn(hidden, down_piece)
+            second = nt(grad_up, up_piece)
+            forward = first if forward is None else forward + first
+            backward = second if backward is None else backward + second
+        sum_start(0, i, backward)
+        sum_start(1, i, forward)
+
+    def keep_sums(k, shift, scale):
+        r.sums[k : k + 1, :] += shift
+        r.sums[k + 1 : k + 2, :] += scale
+
+    def after_feed(i):
+        stream = r.x2[i]
+        grad, shift, scale = norm_backward(stream, mod(5), sum_end(0, i))
+        keep_sums(4, shift, scale)
+        grad = r.buf_b[i, s].astype(f32) + grad
+        r.buf_b2[i, s] = grad.astype(bf16)
+        gather_start(r.buf_b2, i)
+        r.part_side[i, 0, 0] = (r.x2[i] + sum_end(1, i)).astype(bf16)
+        r.x2[i] = grad
+        output_copy(i).start()
+
+    def self_back(i):
+        gather_wait(r.buf_b2, i)
+        grad = nt(r.buf_b2[i].reshape(rows, D), W[OS][...].reshape(C, D)).astype(bf16)
+        attend_back(i, *own, grad, None, r.grad_up)
+
+    def grads_into(place, lhs, rhs, block, width):
+        pieces = 4
+        count = lhs.shape[1] // pieces
+        for k in range(pieces):
+            value = tn(lhs[:, k * count : (k + 1) * count], rhs).astype(bf16)
+            lead = count // block
+            for m in range(lead):
+                o = k * lead + m
+                place[o // 2, o % 2, :, :width] = value[m * block : (m + 1) * block]
+
+    def feed_grads():
+        grads_into(
+            r.grads_b,
+            r.hidden,
+            r.buf_b[...].reshape(z.tokens, D),
+            z.block,
+            D,
+        )
+        grad_start(DOWN)
+        grads_into_blocks(r.grads_a, r.buf_a, r.grad_up, z.hidden)
+        grad_start(UP)
+
+    def grads_into_blocks(place, lhs4, rhs, width):
+        for o in range(B):
+            left = lhs4[:, :, :, o * z.block : (o + 1) * z.block].reshape(z.tokens, z.block)
+            place[o // 2, o % 2, :, :width] = tn(left, rhs[:, :width]).astype(bf16)
+
+    pipeline(
+        (0, self_forward),
+        (1, lambda i: sum_pass(0, i)),
+        (2, after_self),
+        (3, lambda i: gather_pass(r.buf_a, i)),
+        (4, feed),
+        (4, lambda i: at(i, n - 1, feed_grads)),
+        (5, lambda i: (sum_pass(0, i), sum_pass(1, i))),
+        (6, after_feed),
+        (7, lambda i: gather_pass(r.buf_b2, i)),
+        (8, self_back),
+    )
+    grad_pass(DOWN)
+    grad_pass(UP)
+
+    r.grad_up[:, C : 2 * C] = r.grad_key[:, : z.tokens].T.astype(bf16)
+    r.grad_up[:, 2 * C : 3 * C] = r.grad_value[:, : z.tokens].T.astype(bf16)
+
+    clear_keys()
+
+    def self_down(i):
+        sum_start(0, i, nt(r.grad_up[chunk(i), : 3 * C], W[QKV][...].reshape(D, 3 * C)))
+
+        @functools.partial(at, i, 0)
+        def _():
+            value = tn(r.att2[...], r.buf_b2[...].reshape(z.tokens, D)).astype(bf16)
+            r.grads_c[1] = value.reshape(2, z.block, D)
+            grad_start(OS)
+
+        @functools.partial(at, i, n - 1)
+        def _():
+            grads_into_blocks(r.grads_a, r.buf_h2, r.grad_up, 3 * C)
+            grad_start(QKV)
+
+    def after_self_down(i):
+        grad, shift, scale = norm_backward(r.x1[i], mod(3), sum_end(0, i))
+        keep_sums(2, shift, scale)
+        grad = r.x2[i] + grad
+        r.x2[i] = grad
+        r.buf_b[i, s] = grad.astype(bf16)
+        gather_start(r.buf_b, i)
+
+    def cross_back(i):
+        gather_wait(r.buf_b, i)
+        grad = nt(r.buf_b[i].reshape(rows, D), W[OC][...].reshape(C, D)).astype(bf16)
+        attend_back(i, *cross, grad, mask_rows, r.hidden)
+        sum_start(0, i, nt(r.hidden[chunk(i), :C], W[Q][...].reshape(D, C)))
+        at(i, 0, weights_on((grad_pass, OS), (grad_end, DOWN)))
+        at(i, 1, weights_on((grad_end, UP)))
+        at(i, 2, weights_on((grad_pass, QKV)))
+
+    def after_cross_back(i):
+        grad, shift, scale = norm_backward(r.x0[i].astype(f32), mod(1), sum_end(0, i))
+        keep_sums(0, shift, scale)
+        r.x2[i] += grad
+
+    def last_grads():
+        value = tn(r.att1[...], r.buf_b[...].reshape(z.tokens, D)).astype(bf16)
+        r.grads_c[0] = value.reshape(2, z.block, D)
+        grad_start(OC)
+        for side, rest in enumerate((r.grad_key[...], r.grad_value[...])):
+            total = None
+            for _ in range(3):
+                term = rest.astype(bf16)
+                rest = rest - term.astype(f32)
+                product_term = nn(term, r.image_all[...])
+                total = product_term if total is None else total + product_term
+            value = total.T.astype(bf16)
+            for o in range(B):
+                r.grads_b[o // 2, o % 2, : z.image_block, C + side * C : C + (side + 1) * C] = value[
+                    o * z.image_block : (o + 1) * z.image_block
+                ]
+        grad_start(KV)
+        for o in range(B):
+            left = r.normed1[:, o * z.block : (o + 1) * z.block]
+            r.grads_b[o // 2, o % 2, :, :C] = tn(left, r.hidden[:, :C]).astype(bf16)
+        grad_start(Q)
+
+    pipeline(
+        (0, self_down),
+        (1, lambda i: sum_pass(0, i)),
+        (2, after_self_down),
+        (3, lambda i: gather_pass(r.buf_b, i)),
+        (4, cross_back),
+        (4, lambda i: at(i, n - 1, last_grads)),
+        (5, lambda i: sum_pass(0, i)),
+        (6, after_cross_back),
+    )
+    grad_copy = pltpu.make_async_copy(r.x2, r.grad_tokens, r.sem_out.at[7])
+    grad_copy.start()
+
+    def sums_send(j):
+        return remote(
+            r.sums, r.sums_seq.at[s], r.sem_d_s.at[j - 1], r.sem_d_r.at[s], (b, lax.rem(s + j, S))
+        )
+
+    for j in range(1, S):
+        sums_send(j).start()
+    grad_pass(OC)
+    grad_end(OS)
+    grad_end(QKV)
+    total = r.sums[...]
+    for j in range(1, S):
+        k = lax.rem(s + j, S)
+        arrived(r.sums_seq.at[k], r.sem_d_s.at[0], r.sem_d_r.at[k], (b, k))
+        total = total + r.sums_seq[k]
+    r.mods_all[b] = total
+
+    def table_send(j):
+        return remote(
+            r.mods_all.at[b],
+            r.mods_all.at[b],
+            r.sem_t_s.at[j - 1],
+            r.sem_t_r.at[b],
+            (lax.rem(b + j, B), s),
+        )
+
+    for j in range(1, B):
+        table_send(j).start()
+    grad_pass(KV)
+    grad_pass(Q)
+    for j in range(1, B):
+        k = lax.rem(b + j, B)
+        arrived(r.mods_all.at[k], r.sem_t_s.at[0], r.sem_t_r.at[k], (k, s))
+    table_copy = pltpu.make_async_copy(r.mods_all, r.table, r.sem_out.at[8])
+    table_copy.start()
+    grad_end(OC)
+    grad_end(KV)
+    grad_end(Q)
+    for j in range(1, S):
+        sums_send(j).wait_send()
+    for j in range(1, B):
+        table_send(j).wait_send()
+    for w in range(7):
+        weight_drain(w)
+    for w in (DOWN, UP, OS, QKV, OC, KV, Q):
+        grad_drain(w)
+    for i in range(n):
+        output_copy(i).wait()
+    grad_copy.wait()
+    table_copy.wait()
+
+
+def layer_call(z, args):
+    n, part, D, C, S, B = z.chunks, z.part, z.width, z.columns, z.seq, z.batch
+    Z = B // 2
+    own = (n, part, D)
+    full = (n, S, part, D)
+    vmem = pltpu.VMEM
+    dma = pltpu.SemaphoreType.DMA
+    by_rows = (OC, OS)
+    weights = [
+        vmem(((2,) if w in by_rows else (B,)) + shape, bf16) for w, shape in enumerate(z.weights)
+    ]
+    firsts = [
+        vmem((() if w in by_rows else (Z,)) + shape, bf16) for w, shape in enumerate(z.weights)
+    ]
+    seconds = [vmem((Z - 1,) + shape, bf16) for shape in z.weights]
+    lane = [
+        vmem((n, 2, 2, part, D), bf16),
+        vmem((n, 2, part, D), bf16),
+        vmem((n, part, D), bf16),
+        vmem((n, part, D), bf16),
+    ]
+    scratch = (
+        weights
+        + firsts
+        + seconds
+        + [vmem(full, bf16)] * 4
+        + lane
+        + lane
+        + [
+            vmem((z.keys, z.image_width), bf16),
+            vmem((8, z.keys), f32),
+            vmem(args[5].shape, bf16),
+            vmem((B, 8, D), f32),
+            vmem((8, D), f32),
+            vmem((8, D), f32),
+            vmem((S, 8, D), f32),
+            vmem((z.tokens, D), bf16),
+            vmem((z.tokens, C), bf16),
+            vmem((z.keys, C), bf16),
+            vmem((z.keys, C), bf16),
+            vmem((z.tokens, C), bf16),
+            vmem((z.tokens, 3 * C), bf16),
+            vmem((z.tokens, C), bf16),
+            vmem((z.tokens, z.hidden), bf16),
+            vmem((z.tokens, z.hidden), bf16),
+            vmem((C, z.keys), f32),
+            vmem((C, z.keys), f32),
+            vmem(own, bf16),
+            vmem(own, f32),
+            vmem(own, f32),
+            vmem((Z, 2, z.block, D), bf16),
+            vmem((Z, 2, z.block, D), bf16),
+            vmem((2, 2, z.block, D), bf16),
+            dma((33,)),
+            dma((7, 3)),
+            dma((7, Z)),
+            dma((7, Z)),
+            dma((7, Z)),
+            dma((7,)),
+            dma((7,)),
+            dma((7, 3)),
+            dma((7, Z)),
+            dma((7, 3)),
+            dma((7, S)),
+            dma((2, 3)),
+            dma((2, 3)),
+            dma((n, 3)),
+            dma((n, 3)),
+            dma((2, n, 2)),
+            dma((2, n, 2)),
+            dma((B - 1,)),
+            dma((B,)),
+            dma((S - 1,)),
+            dma((S,)),
+            dma((B - 1,)),
+            dma((B,)),
+            dma((9 + n,)),
+        ]
+    )
+    shape = jax.ShapeDtypeStruct
+    outs = [shape(own, bf16), shape(own, f32), shape((B, 8, D), f32)] + [
+        shape((() if w in by_rows else (S,)) + size, bf16) for w, size in enumerate(z.weights)
+    ]
+    anywhere = pl.BlockSpec(memory_space=pl.ANY)
+    return pl.pallas_call(
+        functools.partial(whole_layer, z),
+        out_shape=outs,
+        in_specs=[anywhere] * len(args),
+        out_specs=[anywhere] * len(outs),
+        scratch_shapes=scratch,
+        compiler_params=pltpu.CompilerParams(
+            collective_id=0, has_side_effects=True, vmem_limit_bytes=LIMIT
+        ),
+        name="whole_layer",
+    )(*args)
+
+
+def local_kernel(sizes, *inputs):
+    (
+        tokens,
+        cotangent,
+        image_tokens,
+        image_lengths,
+        key_mask,
+        camera,
+        modulation,
+        q_cross,
+        kv_image,
+        out_cross,
+        qkv_self,
+        out_self,
+        mlp_in,
+        mlp_out,
+    ) = inputs
+    z = sizes
+    n, part, D, C, S, B = z.chunks, z.part, z.width, z.columns, z.seq, z.batch
+    positions = jnp.arange(z.keys, dtype=jnp.int32)
+    marked = jnp.pad(key_mask[0], (0, z.keys - z.image_rows)) == 1
+    valid = (positions < image_lengths[0]) & (marked | (positions == 0))
+    fill = jnp.where(positions < z.image_rows, -1000000000.0, BELOW)
+    mask = jnp.concatenate(
+        [valid.astype(f32)[None], fill[None], jnp.zeros((6, z.keys), f32)], axis=0
+    )
+    tail = jnp.pad(
+        image_tokens[0, z.whole_rows :], ((0, z.keys - z.image_rows), (0, 0))
+    )
+    results = layer_call(
+        z,
+        (
+            tokens[0].reshape(n, part, D),
+            cotangent[0].reshape(n, part, D),
+            image_tokens[0],
+            tail,
+            mask,
+            camera,
+            modulation,
+            q_cross,
+            kv_image,
+            out_cross,
+            qkv_self,
+            out_self,
+            mlp_in,
+            mlp_out,
+        ),
+    )
+    output, grad_tokens, table, *grads = results
+    gate = jax.nn.silu(camera.astype(f32)).astype(bf16).astype(f32)
+    grad_modulation = lax.dot_general(
+        gate,
+        table[:, :6, :].reshape(B, 6 * D),
+        (((0,), (0,)), ((), ())),
+        precision=highest,
+        preferred_element_type=f32,
+    )
+
+    def across(grad, groups):
+        rows, width = grad.shape[1:]
+        split = grad.reshape(S, rows, groups, width // groups).transpose(1, 2, 0, 3)
+        return split.reshape(rows, S * width).astype(f32)
+
+    return (
+        output.reshape(1, z.own, D),
+        grad_tokens.reshape(1, z.own, D),
+        grad_modulation,
+        across(grads[Q], 1),
+        across(grads[KV], 2),
+        grads[OC].astype(f32),
+        across(grads[QKV], 3),
+        grads[OS].astype(f32),
+        across(grads[UP], B),
+        grads[DOWN].reshape(-1, D).astype(f32),
+    )
+
+
+def fits(mesh, inputs):
+    batch, seq = mesh.shape["batch"], mesh.shape["seq"]
+    own, width = inputs[0].shape[1:]
+    return (
+        batch == 8
+        and seq == 4
+        and own % 64 == 0
+        and width == HEADS * HEAD_DIM
+        and (width // seq) % 128 == 0
+        and (inputs[12].shape[1] // seq // batch) % 128 == 0
+    )
+
+
+def choose(mesh, *inputs):
+    if not fits(mesh, inputs):
+        return local(*inputs)
+    return local_kernel(Sizes(mesh.shape, inputs), *inputs)
+
+
 def solution(mesh):
     return jax.shard_map(
-        local,
+        functools.partial(choose, mesh),
         mesh=mesh,
         in_specs=(
             P("batch", "seq", None),

time: 1940 us -> 358 us (0.18)
  waiting for transfers between devices: 1620 us -> 0 us
  Pallas kernels: 0 us -> 330 us
  matrix products: 194 us -> 3.1 us
  local copies, waits for them, and re-layouts: 57.5 us -> 13.5 us
  other arithmetic: 31.7 us -> 5.77 us
    reduce_scatter x11 -> x0, waiting for transfers between devices: 823 us -> none  [the longest x1 154 us: local(): lax.psum_scatter(terms[5].astype(jnp.bfloat16), 'batch', scatter_dimensio...]
    all_gather x9 -> x0, waiting for transfers between devices: 523 us -> none  [the longest x1 122 us: local(): lax.all_gather(mlp_in, 'batch', axis=0, tiled=True)]
    pallas_call x0 -> x1, Pallas kernels: none -> 330 us  [layer_call(): pl.pallas_call(functools.partial(whole_layer, z), out_shape=outs, in_spec...]
    psum x3 -> x0, waiting for transfers between devices: 269 us -> none  [the longest x1 119 us: local(): grad_table = lax.psum(grad_table, ('batch', 'seq'))]
    dot_general x78 -> x1, matrix products: 194 us -> 3.1 us  [local_kernel(): lax.dot_general(gate, table[:, :6, :].reshape(B, 6 * D), (((0,), (0,)), (...]
  transfers between devices with their start and end apart: 23 -> 0, of which waited for: 23 -> 0; matrix products, arithmetic and copies ran while one was open for 8% -> 0% of each run, Pallas kernels for 0% -> 0%
where the time goes in v1:
time: 358 us; the launch traced here: 354 us
  Pallas kernels  330 us (92%)
  local copies, waits for them, and re-layouts  13.5 us (4%)
  other arithmetic  5.77 us (2%)
    pallas_call x1, Pallas kernels, layer_call(): pl.pallas_call(functools.partial(whole_layer, z), out_shape=outs, in_spec...  330 us

profile of v1, /device:TPU:17, one launch (start us, length us, event | category | flops | bytes accessed | tf_op | source)
XLA Modules:
  0.0 353.6 jit_solution(13215819109389190197)
XLA Ops:
  1.4 0.7 slice_bitcast_fusion.1
  2.1 0.7 reduce
  2.8 0.7 maximum_maximum_fusion.refs_4_
  3.5 0.7 pad.8.refs_3_
  4.2 329.6 %whole_layer.1 = (bf16[4,64,1024]{2,1,0:T(8,128)(2,1)}, f32[4,64,1024]{2,1,0:T(8,128)}, f32[8,8,1024]{2,1,0:T(8,128)}, bf16[4,128,256]{2,1,0:T(8,128)(2,1)}, bf1...) custom-call(bf16[4,64,1024]{2,1,0:T(8,128)(2,1)} %bitcast.45, ...), custom_call_target="tpu_custom_call" | custom-call | tf_op jit(solution)/shard_map/whole_layer/pallas_call | solution.py:1379
  333.9 1.0 slice_bitcast_fusion
  335.0 1.0 convert_bitcast_fusion
  336.1 0.2 copy.32
  336.3 1.0 copy.37
  337.3 0.8 convert_element_type.80
  338.1 0.8 convert_element_type.85
  339.0 0.5 reshape.76
  339.5 0.5 copy.33
  340.0 1.3 reshape.71
  341.3 0.3 copy.34
  341.7 1.6 copy.38
  343.3 0.3 copy.40
  343.5 0.1 bitcast_bitcast_fusion
  343.7 1.4 copy.36
  345.1 1.9 reshape.73
  346.9 1.6 bitcast_convert_fusion
  348.6 3.1 fusion.7
  351.7 0.8 copy.44
  352.5 1.0 copy.45
  (25 shorter events, 0.4 us)
Async XLA Ops:
  333.9 3.4 copy-start.7
  334.9 3.2 copy-start.6
  335.0 3.9 %copy-start.5 = (bf16[4,96,512]{2,1,0:T(8,128)(2,1)S(1)}, bf16[4,96,512]{2,1,0:T(8,128)(2,1)}, u32[]{:S(2)}) copy-start(bf16[4,96,512]{2,1,0:T(8,128)(2,1)} %get-tuple-element.24) | copy-start | bytes 1179652
  339.0 2.3 copy-start.3
  341.6 1.6 copy-start.1
  345.0 1.9 copy-start
  346.9 1.6 copy-start.8
  348.5 3.1 copy-start.4
  348.6 3.9 %copy-start.2 = (f32[4,64,1024]{2,1,0:T(8,128)S(1)}, f32[4,64,1024]{2,1,0:T(8,128)}, u32[]{:S(2)}) copy-start(f32[4,64,1024]{2,1,0:T(8,128)} %get-tuple-element.21) | copy-start | bytes 3145732
